TPU v7x, 512 devices: a whole 4x4x16 slice. The times are simulated.
512 devices in a mesh: dp: 32 (over x, y, core), mp: 16 (over z).
Axes of the slice: x: 4, y: 4, z: 16, core: 2. Of those that a mesh axis runs over, the one named last changes fastest.
Arguments:
- patches: bfloat16 [512, 128, 1536], P(('dp', 'mp')), may hold values from -6 to 6
- keep_index: int32 [512, 128], P(('dp', 'mp')), may hold values from 0 to 127, each once within a row
- visible: int32 [512], P(('dp', 'mp')), may hold values from 16 to 80, as said below
- targets: bfloat16 [512, 12288], P(('dp', 'mp')), may hold values from -6 to 6
- w_up: bfloat16 [1536, 6144], P(None, 'mp'), may hold values from -0.15625 to 0.15625
- w_down: bfloat16 [6144, 1536], P('mp'), may hold values from -0.078125 to 0.078125
- dec_embed: bfloat16 [1536, 512], P('mp'), may hold values from -0.15625 to 0.15625
- dec_qkv: bfloat16 [512, 1536], P('mp'), may hold values from -1.45840774 to 1.45840774
- dec_out: bfloat16 [512, 512], P('mp'), may hold values from -0.25 to 0.25
- dec_pred: bfloat16 [512, 96], P('mp'), may hold values from -0.25 to 0.25
- mask_token: bfloat16 [512], replicated, may hold values from -4 to 4
- position: bfloat16 [128, 512], replicated, may hold values from -4.5 to 4.5
Outputs:
- recon: bfloat16 [512, 12288], P(('dp', 'mp'))
- patch_loss: float32 [512, 128], P(('dp', 'mp'))
Inputs may be any that keep to these rules, and one draw needn't show every extreme that they name: For c < 256, visible[c] + visible[c + 256] = 96; some crop has exactly 80 visible patches.
All inputs are finite; a program needn't handle non-finite values.
Results may differ from a plain program's by a relative error of at most 0.04.
Values may be sent and summed in bfloat16 or wider, within the bound.
A program may use at most 64 MiB of HBM per device.

v0:
```python
import math

import jax
import jax.numpy as jnp
from jax import lax
from jax.sharding import PartitionSpec as P

DD = 512
HSIZE = 64
PIX = 96
VMAX = 80


EPSILON = 1e-06


def layer_norm(values):
    center = values - jnp.mean(values, axis=-1, keepdims=True)
    spread = jnp.mean(center * center, axis=-1, keepdims=True)
    return center * lax.rsqrt(spread + EPSILON)


def encode(row_block, w_up, w_down):
    normed = layer_norm(row_block.astype(jnp.float32)).astype(jnp.bfloat16)
    hidden = jax.nn.gelu(
        jnp.dot(
            lax.all_gather(normed, "mp", axis=0, tiled=True),
            w_up,
            preferred_element_type=jnp.float32,
        ),
        approximate=True,
    ).astype(jnp.bfloat16)
    row_count = row_block.shape[0]
    summed = lax.psum(
        jnp.dot(hidden, w_down, preferred_element_type=jnp.float32).astype(jnp.bfloat16), "mp"
    ).astype(jnp.float32)
    own_sum = lax.dynamic_slice_in_dim(summed, lax.axis_index("mp") * row_count, row_count, 0)
    return (row_block.astype(jnp.float32) + own_sum).astype(jnp.bfloat16)


def body(
    patches,
    keep_index,
    visible,
    targets,
    w_up,
    w_down,
    dec_embed,
    dec_qkv,
    dec_out,
    dec_pred,
    mask_token,
    position,
):
    crop_dev, patch_count, width = patches.shape
    full_embed, full_qkv, full_out, full_pred = (
        lax.all_gather(dec_embed, "mp", axis=0, tiled=True),
        lax.all_gather(dec_qkv, "mp", axis=0, tiled=True),
        lax.all_gather(dec_out, "mp", axis=0, tiled=True),
        lax.all_gather(dec_pred, "mp", axis=0, tiled=True),
    )
    flat_rows = patches.reshape(crop_dev * patch_count, width)
    slots = jnp.arange(patch_count, dtype=jnp.int32)
    matches = keep_index[:, :, None] == slots[None, None, :]
    inverse = jnp.sum(jnp.where(matches, slots[None, :, None], 0), axis=1)
    is_visible = inverse < visible[:, None]
    crop_base = jnp.arange(crop_dev, dtype=jnp.int32) * patch_count
    chosen = keep_index[:, :VMAX] + crop_base[:, None]
    enc_input = jnp.take(flat_rows, chosen.reshape(-1), axis=0)
    encoded = encode(enc_input, w_up, w_down)
    row_index = (jnp.arange(crop_dev, dtype=jnp.int32) * VMAX)[:, None] + jnp.minimum(
        inverse, VMAX - 1
    )
    arrived = jnp.take(encoded, row_index.reshape(-1), axis=0)
    embedded = jnp.dot(arrived, full_embed, preferred_element_type=jnp.float32).astype(jnp.bfloat16)
    heads = DD // HSIZE
    scale = 1.0 / math.sqrt(HSIZE)
    embedded = embedded.reshape(crop_dev, patch_count, DD).astype(jnp.float32)
    start = (
        jnp.where(is_visible[:, :, None], embedded, mask_token.astype(jnp.float32)[None, None, :])
        + position.astype(jnp.float32)[None]
    )
    dec_normed = layer_norm(start).astype(jnp.bfloat16)
    projections = jnp.einsum(
        "kpd,de->kpe", dec_normed, full_qkv, preferred_element_type=jnp.float32
    ).astype(jnp.bfloat16)
    query = projections[:, :, :DD].reshape(crop_dev, patch_count, heads, HSIZE)
    keys = projections[:, :, DD : 2 * DD].reshape(crop_dev, patch_count, heads, HSIZE)
    values = projections[:, :, 2 * DD :].reshape(crop_dev, patch_count, heads, HSIZE)
    scores = jnp.einsum("kqhe,kshe->khqs", query, keys, preferred_element_type=jnp.float32) * scale
    scores = scores - jnp.max(scores, axis=-1, keepdims=True)
    weights = jnp.exp(scores)
    probs = (weights / jnp.sum(weights, axis=-1, keepdims=True)).astype(jnp.bfloat16)
    mixed = jnp.einsum("khqs,kshe->kqhe", probs, values, preferred_element_type=jnp.float32)
    mixed = mixed.astype(jnp.bfloat16).reshape(crop_dev, patch_count, DD)
    after = start + jnp.einsum("kpd,de->kpe", mixed, full_out, preferred_element_type=jnp.float32)
    final = layer_norm(after).astype(jnp.bfloat16)
    prediction = jnp.einsum("kpd,de->kpe", final, full_pred, preferred_element_type=jnp.float32)
    error = prediction - targets.reshape(crop_dev, patch_count, PIX).astype(jnp.float32)
    patch_loss = jnp.where(
        is_visible, jnp.zeros(is_visible.shape, jnp.float32), jnp.mean(error * error, axis=-1)
    )
    recon = prediction.astype(jnp.bfloat16).reshape(crop_dev, patch_count * PIX)
    return (recon, patch_loss)


def solution(mesh):
    return jax.shard_map(
        body,
        mesh=mesh,
        in_specs=(
            P(("dp", "mp"), None, None),
            P(("dp", "mp"), None),
            P(("dp", "mp")),
            P(("dp", "mp"), None),
            P(None, "mp"),
            P("mp", None),
            P("mp", None),
            P("mp", None),
            P("mp", None),
            P("mp", None),
            P(),
            P(),
        ),
        out_specs=(P(("dp", "mp"), None), P(("dp", "mp"), None)),
        check_vma=False,
    )
```

profile of v0, /device:TPU:6, one launch (start us, length us, event | category | flops | bytes accessed | tf_op | source)
XLA Modules:
  0.0 410.7 jit_solution(13631584163739360599)
XLA Ops:
  7.2 0.0 copy-start
  7.2 0.0 copy-start.5
  7.2 0.0 all-gather.4.cloned.1.call-start
  7.2 0.8 fusion.33
  8.0 0.7 compare_and_fusion
  8.7 2.0 gather_fusion
  10.8 0.2 convert_reduce_fusion
  11.0 0.2 fusion.22
  11.2 0.9 fusion.23
  12.1 0.0 all-gather.4.cloned.1.call-update
  12.1 0.0 all-reduce.2.cloned.1.call-start
  12.2 82.5 %all-gather.4.cloned.1.call-done = bf16[1280,1536]{1,0:T(8,128)(2,1)} async-done(((bf16[80,1536]{1,0:T(8,128)(2,1)}), bf16[1280,1536]{1,0:T(8,128)(2,1)}) %all-gather.4.cloned.1.call-update) | async-done | bytes 3932176 | tf_op jit(solution)/shard_map/all_gather | solution.py:27
  94.7 0.0 copy-done
  94.7 0.0 copy-done.5
  94.7 8.6 %convolution_convert_fusion = bf16[1280,1536]{1,0:T(8,128)(2,1)} fusion(bf16[384,1536]{1,0:T(8,128)(2,1)S(1)} %copy-done, bf16[1280,1536]{1,0:T(8,128)(2,1)} %all-gather.4.cloned.1.call-done, bf16[1536,384]{1,0:T(8,128)(2,1)S(1)} %copy-done.5), kind=kOutput, calls=%fused_computation.3 | convolution fusion | flops 3026288640 | bytes 10223616 | tf_op jit(solution)/shard_map/dot_general | solution.py:35
  103.2 0.0 copy-start.2
  103.3 0.0 all-reduce.2.cloned.1.call-update
  103.3 0.0 all-gather.6.cloned.1.call-start
  103.3 0.7 all-gather.6.cloned.1.call-update
  104.0 0.0 all-gather.8.cloned.1.call-start
  104.1 0.5 all-gather.8.cloned.1.call-update
  105.2 0.0 copy-done.4
  105.3 0.1 convert_reduce_fusion.1
  105.4 0.1 reshape.303
  105.5 0.1 copy.29
  105.6 29.5 %all_gather.19 = bf16[512,96]{1,0:T(8,128)(2,1)S(1)} all-gather(bf16[32,96]{1,0:T(8,128)(2,1)S(1)} %copy-done.3), channel_id=1, replica_groups=mesh['dp'=32,'mp'=16] {'mp'}, dimensions={0}, use_global_device_ids=true | all-gather | bytes 104448 | tf_op jit(solution)/shard_map/all_gather | solution.py:60
  135.1 0.1 select_reduce_fusion
  135.3 31.5 %all_gather.18 = bf16[512,512]{1,0:T(8,128)(2,1)S(1)} all-gather(bf16[32,512]{1,0:T(8,128)(2,1)S(1)} %copy-done.2), channel_id=1, replica_groups=mesh['dp'=32,'mp'=16] {'mp'}, dimensions={0}, use_global_device_ids=true | all-gather | bytes 557056 | tf_op jit(solution)/shard_map/all_gather | solution.py:59
  166.8 89.7 %all-reduce.2.cloned.1.call-done = bf16[1280,1536]{1,0:T(8,128)(2,1)} async-done(((bf16[1280,1536]{1,0:T(8,128)(2,1)}), bf16[1280,1536]{1,0:T(8,128)(2,1)}) %all-reduce.2.cloned.1.call-update) | async-done | bytes 3932176 | tf_op jit(solution)/shard_map/psum | solution.py:34
  256.5 1.1 fusion.24
  257.6 0.9 gather_fusion.1
  258.5 68.8 %all-gather.6.cloned.1.call-done = bf16[1536,512]{1,0:T(8,128)(2,1)} async-done(((bf16[96,512]{1,0:T(8,128)(2,1)}), bf16[1536,512]{1,0:T(8,128)(2,1)}) %all-gather.6.cloned.1.call-update) | async-done | bytes 1572880 | tf_op jit(solution)/shard_map/all_gather | solution.py:57
  327.3 1.9 fusion.43
  329.2 0.2 multiply_reduce_fusion.1
  329.4 69.3 %all-gather.8.cloned.1.call-done = bf16[512,1536]{1,0:T(8,128)(2,1)} async-done(((bf16[32,1536]{1,0:T(8,128)(2,1)}), bf16[512,1536]{1,0:T(8,128)(2,1)}) %all-gather.8.cloned.1.call-update) | async-done | bytes 1572880 | tf_op jit(solution)/shard_map/all_gather | solution.py:58
  398.7 1.8 fusion.1
  400.6 0.1 copy.25
  400.7 0.1 copy.26
  400.9 0.3 convolution_multiply_fusion
  401.2 0.4 fusion.44
  401.5 0.1 copy.24
  401.7 0.3 convolution_convert_fusion.2
  401.9 0.3 fusion.45
  402.3 0.2 multiply_reduce_fusion
  402.5 0.3 multiply_reduce_fusion.2
  402.8 0.1 copy.28
  402.9 0.7 reshape.302
  403.6 0.5 select_bitcast_fusion
  (22 shorter events, 0.1 us)
Async XLA Ops:
  7.2 87.5 %copy-start = (bf16[384,1536]{1,0:T(8,128)(2,1)S(1)}, bf16[384,1536]{1,0:T(8,128)(2,1)}, u32[]{:S(2)}) copy-start(bf16[384,1536]{1,0:T(8,128)(2,1)} %param.17) | copy-start | bytes 3538948
  7.2 87.5 %copy-start.5 = (bf16[1536,384]{1,0:T(8,128)(2,1)S(1)}, bf16[1536,384]{1,0:T(8,128)(2,1)}, u32[]{:S(2)}) copy-start(bf16[1536,384]{1,0:T(8,128)(2,1)} %param.16) | copy-start | bytes 3538948
  7.2 87.5 %all-gather.4.cloned.1.call-start = ((), (), s32[]{:S(2)}) async-start(), calls=%async_computation | async-start | bytes 4177920 | tf_op jit(solution)/shard_map/all_gather | solution.py:27
  12.1 244.4 %all-reduce.2.cloned.1.call-start = ((), (), s32[]{:S(2)}) async-start(), calls=%async_computation.1 | async-start | bytes 7864320 | tf_op jit(solution)/shard_map/psum | solution.py:34
  103.2 2.0 copy-start.4
  103.2 2.0 copy-start.1
  103.2 2.3 copy-start.3
  103.2 31.9 %copy-start.7 = (s32[1,128]{1,0:T(1,128)S(1)}, s32[1,128]{1,0:T(1,128)}, u32[]{:S(2)}) copy-start(s32[1,128]{1,0:T(1,128)} %param.13) | copy-start | bytes 1540
  103.2 32.0 %copy-start.2 = (bf16[32,512]{1,0:T(8,128)(2,1)S(1)}, bf16[32,512]{1,0:T(8,128)(2,1)}, u32[]{:S(2)}) copy-start(bf16[32,512]{1,0:T(8,128)(2,1)} %param.20) | copy-start | bytes 98308
  103.3 224.0 %all-gather.6.cloned.1.call-start = ((), (), s32[]{:S(2)}) async-start(), calls=%async_computation.2 | async-start | bytes 1671168 | tf_op jit(solution)/shard_map/all_gather | solution.py:57
  104.0 294.7 %all-gather.8.cloned.1.call-start = ((), (), s32[]{:S(2)}) async-start(), calls=%async_computation.3 | async-start | bytes 1671168 | tf_op jit(solution)/shard_map/all_gather | solution.py:58
  166.8 160.5 %copy-start.6 = (bf16[128,512]{1,0:T(8,128)(2,1)S(1)}, bf16[128,512]{1,0:T(8,128)(2,1)}, u32[]{:S(2)}) copy-start(bf16[128,512]{1,0:T(8,128)(2,1)} %param.23) | copy-start | bytes 393220
Sparse Core Ops, SparseCore 0:
  12.2 82.3 all-gather.3
  103.4 153.0 all-reduce.1
  258.8 68.4 all-gather.5
  329.4 69.2 all-gather.7
where the time goes:
time: 411 us
  waiting for transfers between devices  312 us (76%)
  blocking collectives  61.1 us (15%)
  between operations  14.6 us (4%)
  matrix products  13.8 us (3%)
  other arithmetic  5.06 us (1%)
  local copies, waits for them, and re-layouts  4.4 us (1%)
    psum x1, waiting for transfers between devices, encode(): lax.psum(jnp.dot(hidden, w_down, preferred_element_type=jnp.float32).asty...  89.7 us
    all_gather x1, waiting for transfers between devices, encode(): lax.all_gather(normed, 'mp', axis=0, tiled=True)  82.5 us
    all_gather x1, waiting for transfers between devices, body(): lax.all_gather(dec_qkv, 'mp', axis=0, tiled=True)  69.3 us
    all_gather x1, waiting for transfers between devices, body(): lax.all_gather(dec_embed, 'mp', axis=0, tiled=True)  68.8 us
    all_gather x1, blocking collectives, body(): lax.all_gather(dec_out, 'mp', axis=0, tiled=True)  31.5 us
    all_gather x1, blocking collectives, body(): lax.all_gather(dec_pred, 'mp', axis=0, tiled=True)  29.5 us
    dot_general x1, matrix products, encode(): jnp.dot(hidden, w_down, preferred_element_type=jnp.float32)  8.55 us
  transfers between devices with their start and end apart: 4, of which 4 were waited for; matrix products, arithmetic and copies ran while one was open for 1% of the time, Pallas kernels for 0%

commit v1 on v0

v1 whole, which is shorter than its diff:
```python
import functools
import math

import jax
import jax.numpy as jnp
from jax import lax
from jax.experimental import pallas as pl
from jax.experimental.pallas import tpu as pltpu
from jax.sharding import PartitionSpec as P

D = 1536
DD = 512
HSIZE = 64
PIX = 96
VMAX = 80
N_PATCH = 128
NZ = 16
SHARD = 384
LANES = 128
EPSILON = 1e-06
MESH = pl.DeviceIdType.MESH
F32 = jnp.float32
BF16 = jnp.bfloat16

EMBED_AT = 0
QKV_AT = 384
OUT_AT = 768
PRED_AT = 896
PACKED = 1024

UP_PIECE = 48
DOWN_PIECE = 144
CHUNKS = ((0, 48), (48, 32))


def z_slot(z):
    return (z % 4) * 4 + z // 4


def layer_norm(values):
    center = values - jnp.mean(values, axis=-1, keepdims=True)
    spread = jnp.mean(center * center, axis=-1, keepdims=True)
    return center * lax.rsqrt(spread + EPSILON)


def gelu(v):
    return 0.5 * v * (1.0 + jnp.tanh(math.sqrt(2.0 / math.pi) * (v + 0.044715 * v * v * v)))


def dot(a, b):
    return jnp.dot(a, b, preferred_element_type=F32)


def kernel(
    visible, keep_col, keep_row, patches, targets, mask_token, position,
    w_up, w_down, d_embed, d_qkv, d_out, d_pred,
    recon, loss,
    up, down, packed, up2, down2, dec, raw, slots, hidden, w2e, part, own, ret_out, ret_in, proj, mixed,
    load_sem, w_send, w_recv, d_send, d_recv, r_send, r_recv, b_send, b_recv,
):
    dp, z = lax.axis_index("dp"), lax.axis_index("mp")
    x, y, c = dp // 8, (dp // 2) % 4, dp % 2
    sign = 1 - 2 * c
    q_x = c * 16 + y * 4 + x
    q_y = c * 16 + x * 4 + y
    cls = z % 4
    q_z = jnp.where(cls < 2, q_x, q_y)

    def at_z(step):
        return (dp, (z + step + 2 * NZ) % NZ)

    def at_x(step):
        return (((x + step) % 4) * 8 + y * 2 + c, z)

    def at_y(step):
        return (x * 8 + ((y + step) % 4) * 2 + c, z)

    other_core = (x * 8 + y * 2 + (1 - c), z)
    ahead, behind = at_z(sign), at_z(-sign)

    barrier = pltpu.get_barrier_semaphore()
    greeted = [at_z(s) for s in (1, 2, 3, 4, 8, 12, 15)]
    greeted += [at_x(s) for s in (1, 2, 3)] + [at_y(s) for s in (1, 2, 3)] + [other_core]
    greeted_back = [at_z(s) for s in (13, 14)]
    for device in greeted + greeted_back:
        pl.semaphore_signal(barrier, inc=1, device_id=device, device_id_type=MESH)

    loads = []

    def load(src, dst):
        copy = pltpu.make_async_copy(src, dst, load_sem.at[len(loads)])
        copy.start()
        loads.append(copy)

    for j in range(4):
        load(d_embed.at[:, pl.ds(j * LANES, LANES)], packed.at[pl.ds(EMBED_AT + j * 96, 96)])
    for j in range(12):
        load(d_qkv.at[:, pl.ds(j * LANES, LANES)], packed.at[pl.ds(QKV_AT + j * 32, 32)])
    for j in range(4):
        load(d_out.at[:, pl.ds(j * LANES, LANES)], packed.at[pl.ds(OUT_AT + j * 32, 32)])
    load(d_pred, packed.at[pl.ds(PRED_AT, 32)])
    load(w_up, up)
    for j in range(12):
        load(w_down.at[:, pl.ds(j * LANES, LANES)], down.at[pl.ds(j * SHARD, SHARD)])
    packed[pl.ds(PRED_AT + 32, PACKED - PRED_AT - 32), :] = jnp.zeros((PACKED - PRED_AT - 32, LANES), BF16)

    chosen = keep_col[0:VMAX, :] == lax.broadcasted_iota(jnp.int32, (VMAX, N_PATCH), 1)
    picked = dot(chosen.astype(F32).astype(BF16), patches[...])
    raw[...] = picked.astype(BF16)
    slots[0] = layer_norm(picked).astype(BF16)

    for copy in loads:
        copy.wait()
    pl.semaphore_wait(barrier, len(greeted) + len(greeted_back))

    def send(src, dst, sems, index, device):
        copy = pltpu.make_async_remote_copy(
            src_ref=src, dst_ref=dst, send_sem=sems[0].at[index], recv_sem=sems[1].at[index],
            device_id=device, device_id_type=MESH,
        )
        copy.start()
        return copy

    sent = []

    def send_all(items, sems, first):
        copies = [send(src, dst, sems, first + i, device) for i, (src, dst, device) in enumerate(items)]
        sent.extend(copies)
        return copies

    def arrive(copies):
        for copy in copies:
            copy.wait_recv()

    wsem, dsem, rsem, bsem = (w_send, w_recv), (d_send, d_recv), (r_send, r_recv), (b_send, b_recv)

    def up_at(piece, count):
        return pl.ds(pl.multiple_of(piece * UP_PIECE, 16), count * UP_PIECE)

    def down_at(piece, count):
        return pl.ds(pl.multiple_of(piece * DOWN_PIECE, 16), count * DOWN_PIECE)

    w0 = send_all(
        [
            (up.at[up_at(q_x, 1)], up2.at[up_at(q_x, 1)], at_z(8)),
            (down.at[down_at(q_y, 1)], down2.at[down_at(q_y, 1)], at_z(8)),
        ],
        wsem, 0,
    )

    def rows_at(piece, count):
        return pl.ds(pl.multiple_of(piece * 32, 32), count * 32)

    mine = z_slot(z)
    dec[mine, rows_at(q_z, 1), :] = packed[rows_at(q_z, 1), :]
    d0 = send_all(
        [(packed.at[rows_at(q_z, 1)], dec.at[mine, rows_at(q_z, 1)], at_z(s)) for s in (4, 8, 12)], dsem, 0
    )

    def send_rows(k, side):
        first = 0 if side == 0 else 3
        src = 0 if k == 1 else first + k - 1
        dst = first + k
        return [
            (slots.at[src, pl.ds(at, n)], slots.at[dst, pl.ds(at, n)], ahead if side == 0 else behind)
            for at, n in CHUNKS
        ]

    def row_sem(k, side):
        return 2 * ((0 if side == 0 else 3) + k - 1)

    rows = {}

    def start_rows(k, side):
        rows[k, side] = send_all(send_rows(k, side), rsem, row_sem(k, side))

    def pass_rows(k):
        todo = [side for side in (0, 1) if (k, side) in rows]
        items = {side: send_rows(k + 1, side) for side in todo if k + 1 <= (3, 4)[side]}
        for side in items:
            rows[k + 1, side] = []
        for i in range(len(CHUNKS)):
            for side in todo:
                rows[k, side][i].wait_recv()
                if side in items:
                    rows[k + 1, side] += send_all([items[side][i]], rsem, row_sem(k + 1, side) + i)

    start_rows(1, 0)
    start_rows(1, 1)

    def hide(slot):
        hidden[slot, :, 0:SHARD] = gelu(dot(slots[slot], up[...])).astype(BF16)

    hide(0)

    arrive(d0)
    block = pl.ds(pl.multiple_of(cls * 4, 4), 4)
    d1 = send_all(
        [(dec.at[block, rows_at(q_z, 1)], dec.at[block, rows_at(q_z, 1)], at_z(s)) for s in (1, 2, 3)], dsem, 3
    )

    pass_rows(1)
    arrive(w0)
    w1 = send_all(
        [(up2.at[up_at(q_x, 1)], up2.at[up_at(q_x, 1)], at_x(s)) for s in (1, 2, 3)]
        + [(down2.at[down_at(q_y, 1)], down2.at[down_at(q_y, 1)], at_y(s)) for s in (1, 2, 3)],
        wsem, 2,
    )
    hide(1)
    hide(4)

    arrive(d1)
    low, high = pl.ds(0, 8), pl.ds(8, 8)
    d2 = send_all(
        [(dec.at[low, rows_at(q_x, 1)], dec.at[low, rows_at(q_x, 1)], at_x(s)) for s in (1, 2, 3)]
        + [(dec.at[high, rows_at(q_y, 1)], dec.at[high, rows_at(q_y, 1)], at_y(s)) for s in (1, 2, 3)],
        dsem, 6,
    )

    arrive(w1)
    q_xs, q_ys = c * 16 + y * 4, c * 16 + x * 4
    w2 = send_all(
        [(up2.at[up_at(q_xs, 4)], up2.at[up_at(q_xs, 4)], at_y(s)) for s in (1, 2, 3)]
        + [(down2.at[down_at(q_ys, 4)], down2.at[down_at(q_ys, 4)], at_x(s)) for s in (1, 2, 3)],
        wsem, 8,
    )

    pass_rows(2)
    hide(2)
    hide(5)

    arrive(d2)
    d3 = send_all(
        [(dec.at[low, rows_at(q_xs, 4)], dec.at[low, rows_at(q_xs, 4)], at_y(s)) for s in (1, 2, 3)]
        + [(dec.at[high, rows_at(q_ys, 4)], dec.at[high, rows_at(q_ys, 4)], at_x(s)) for s in (1, 2, 3)],
        dsem, 12,
    )

    arrive(w2)
    w3 = send_all(
        [
            (up2.at[up_at(c * 16, 16)], up2.at[up_at(c * 16, 16)], other_core),
            (down2.at[down_at(c * 16, 16)], down2.at[down_at(c * 16, 16)], other_core),
        ],
        wsem, 14,
    )

    pass_rows(3)
    hide(3)
    hide(6)

    arrive(d3)
    d4 = send_all([(dec.at[:, rows_at(c * 16, 16)], dec.at[:, rows_at(c * 16, 16)], other_core)], dsem, 18)

    def weight(at, rows_per, blocks):
        return jnp.concatenate(
            [
                jnp.concatenate(
                    [dec[z_slot(s), at + b * rows_per : at + (b + 1) * rows_per, :] for s in range(NZ)], axis=0
                )
                for b in blocks
            ],
            axis=1,
        )

    pass_rows(4)
    hide(7)
    arrive(w3)

    def hide_far(slot, carry):
        hidden[slot, :, SHARD : 2 * SHARD] = gelu(dot(slots[slot], up2[...])).astype(BF16)
        return carry

    lax.fori_loop(0, 8, hide_far, 0)

    arrive(d4)
    downs = [
        jnp.concatenate([ref[j * SHARD : (j + 1) * SHARD, :] for j in range(12)], axis=1) for ref in (down, down2)
    ]
    for half in (0, 1):
        embed = weight(EMBED_AT, 96, (2 * half, 2 * half + 1))
        cols = slice(256 * half, 256 * half + 256)
        for s in (0, 1):
            w2e[s * SHARD : (s + 1) * SHARD, cols] = dot(downs[s], embed).astype(BF16)
        own[:, cols] = dot(raw[...], embed)

    def partial(slot):
        return dot(hidden[slot], w2e[...])

    ret_out[3] = partial(7).astype(BF16)
    back = {(1, 0): send_all([(ret_out.at[3], ret_in.at[3], ahead)], bsem, 3)}
    ret_out[0] = partial(3).astype(BF16)
    back[0, 0] = send_all([(ret_out.at[0], ret_in.at[0], behind)], bsem, 0)
    own[...] += partial(0)

    def add_part(slot, carry):
        part[slot] = partial(slot)
        return carry

    lax.fori_loop(1, 7, add_part, 0)
    for step in (0, 1, 2):
        arrive(back[1, step])
        ret_out[4 + step] = (ret_in[3 + step].astype(F32) + part[6 - step]).astype(BF16)
        back[1, step + 1] = send_all([(ret_out.at[4 + step], ret_in.at[4 + step], ahead)], bsem, 4 + step)
        if step < 2:
            arrive(back[0, step])
            ret_out[1 + step] = (ret_in[step].astype(F32) + part[2 - step]).astype(BF16)
            back[0, step + 1] = send_all([(ret_out.at[1 + step], ret_in.at[1 + step], behind)], bsem, 1 + step)
    arrive(back[0, 2])
    arrive(back[1, 3])
    embedded = (own[...] + ret_in[2].astype(F32) + ret_in[6].astype(F32)).astype(BF16)

    count = visible[0]
    spread = (keep_row[...] == lax.broadcasted_iota(jnp.int32, (N_PATCH, N_PATCH), 0)) & (
        lax.broadcasted_iota(jnp.int32, (N_PATCH, N_PATCH), 1) < count
    )
    spread = jnp.where(spread, 1.0, 0.0)
    seen = jnp.sum(spread, axis=1, keepdims=True) > 0.5
    placed = dot(spread[:, 0:VMAX].astype(BF16), embedded)
    start = jnp.where(seen, placed, mask_token[...].astype(F32)) + position[...].astype(F32)
    normed = layer_norm(start).astype(BF16)
    for b in range(6):
        both = dot(normed, weight(QKV_AT, 32, (2 * b, 2 * b + 1))).astype(BF16)
        proj[2 * b] = both[:, 0:LANES]
        proj[2 * b + 1] = both[:, LANES : 2 * LANES]
    left = lax.broadcasted_iota(jnp.int32, (N_PATCH, LANES), 1) < HSIZE
    for b in range(4):
        query, keys, values = proj[b], proj[4 + b], proj[8 + b]
        outs = []
        for side in (left, jnp.logical_not(left)):
            one = jnp.where(side, query.astype(F32), 0.0).astype(BF16)
            scores = lax.dot_general(one, keys, (((1,), (1,)), ((), ())), preferred_element_type=F32)
            scores = scores * (1.0 / math.sqrt(HSIZE))
            weights = jnp.exp(scores - jnp.max(scores, axis=-1, keepdims=True))
            probs = (weights / jnp.sum(weights, axis=-1, keepdims=True)).astype(BF16)
            outs.append(dot(probs, values))
        mixed[:, b * LANES : (b + 1) * LANES] = jnp.where(left, outs[0], outs[1]).astype(BF16)
    after = start + jnp.concatenate(
        [dot(mixed[...], weight(OUT_AT, 32, (2 * b, 2 * b + 1))) for b in range(2)], axis=1
    )
    final = layer_norm(after).astype(BF16)
    prediction = dot(final, weight(PRED_AT, 32, (0,)))
    recon[...] = prediction.astype(BF16)
    error = prediction - targets[...].astype(F32)
    error = jnp.sum(error * error, axis=-1, keepdims=True) * (1.0 / PIX)
    loss[...] = jnp.where(seen, 0.0, error)

    for copy in sent:
        copy.wait_send()


def body(
    patches, keep_index, visible, targets, w_up, w_down, dec_embed, dec_qkv, dec_out, dec_pred, mask_token, position
):
    any_spec = pl.BlockSpec(memory_space=pl.ANY)
    vmem = pl.BlockSpec(memory_space=pltpu.VMEM)
    dma = pltpu.SemaphoreType.DMA
    recon, loss = pl.pallas_call(
        kernel,
        out_shape=(
            jax.ShapeDtypeStruct((N_PATCH, LANES), BF16),
            jax.ShapeDtypeStruct((N_PATCH, 1), F32),
        ),
        in_specs=[pl.BlockSpec(memory_space=pltpu.SMEM)] + [vmem] * 6 + [any_spec] * 6,
        out_specs=(vmem, vmem),
        scratch_shapes=[
            pltpu.VMEM((D, SHARD), BF16),
            pltpu.VMEM((12 * SHARD, LANES), BF16),
            pltpu.VMEM((PACKED, LANES), BF16),
            pltpu.VMEM((D, SHARD), BF16),
            pltpu.VMEM((12 * SHARD, LANES), BF16),
            pltpu.VMEM((NZ, PACKED, LANES), BF16),
            pltpu.VMEM((VMAX, D), BF16),
            pltpu.VMEM((8, VMAX, D), BF16),
            pltpu.VMEM((8, VMAX, 2 * SHARD), BF16),
            pltpu.VMEM((2 * SHARD, DD), BF16),
            pltpu.VMEM((8, VMAX, DD), F32),
            pltpu.VMEM((VMAX, DD), F32),
            pltpu.VMEM((7, VMAX, DD), BF16),
            pltpu.VMEM((7, VMAX, DD), BF16),
            pltpu.VMEM((12, N_PATCH, LANES), BF16),
            pltpu.VMEM((N_PATCH, DD), BF16),
            dma((34,)),
            dma((16,)),
            dma((16,)),
            dma((19,)),
            dma((19,)),
            dma((14,)),
            dma((14,)),
            dma((7,)),
            dma((7,)),
        ],
        compiler_params=pltpu.CompilerParams(
            collective_id=0, has_side_effects=True, vmem_limit_bytes=48 * 1024 * 1024
        ),
    )(
        visible,
        keep_index.reshape(N_PATCH, 1),
        keep_index,
        patches.reshape(N_PATCH, D),
        jnp.pad(targets.reshape(N_PATCH, PIX), ((0, 0), (0, LANES - PIX))),
        mask_token.reshape(1, DD),
        position,
        w_up,
        w_down,
        dec_embed,
        dec_qkv,
        dec_out,
        jnp.pad(dec_pred, ((0, 0), (0, LANES - PIX))),
    )
    return (recon[:, :PIX].reshape(1, N_PATCH * PIX), loss.reshape(1, N_PATCH))


def solution(mesh):
    return jax.shard_map(
        body,
        mesh=mesh,
        in_specs=(
            P(("dp", "mp"), None, None),
            P(("dp", "mp"), None),
            P(("dp", "mp")),
            P(("dp", "mp"), None),
            P(None, "mp"),
            P("mp", None),
            P("mp", None),
            P("mp", None),
            P("mp", None),
            P("mp", None),
            P(),
            P(),
        ),
        out_specs=(P(("dp", "mp"), None), P(("dp", "mp"), None)),
        check_vma=False,
    )
```

time: 411 us -> 96.4 us (0.23)
  the two profiles are of different devices: /device:TPU:6 before, /device:TPU:1 now
where the time goes in v1:
time: 96.4 us; the launch traced here: 95.9 us
  Pallas kernels  82.4 us (85%)
  local copies, waits for them, and re-layouts  10.6 us (11%)
  other arithmetic  1.56 us (2%)
  between operations  1.31 us (1%)
    pallas_call x1, Pallas kernels, body(): pl.pallas_call(kernel, out_shape=(jax.ShapeDtypeStruct((N_PATCH, LANES),...  82.4 us
    unnamed x16, local copies, waits for them, and re-layouts  7.63 us

profile of v1, /device:TPU:1, one launch (start us, length us, event | category | flops | bytes accessed | tf_op | source)
XLA Modules:
  0.0 95.9 jit_solution(4276944510312717231)
XLA Ops:
  1.3 0.7 reshape.25.mask_token
  2.0 0.7 pad.9.d_pred
  2.7 0.9 reduce
  3.6 0.1 reshape.24
  3.7 0.8 copy.15.keep_col
  4.5 0.0 copy-start
  4.5 1.3 %copy-done = bf16[1536,384]{1,0:T(8,128)(2,1)S(1)} copy-done((bf16[1536,384]{1,0:T(8,128)(2,1)S(1)}, bf16[1536,384]{1,0:T(8,128)(2,1)}, u32[]{:S(2)}) %copy-start) | copy-done | bytes 1179672
  5.7 0.0 copy-start.1
  5.7 1.3 %copy-done.1 = bf16[384,1536]{1,0:T(8,128)(2,1)S(1)} copy-done((bf16[384,1536]{1,0:T(8,128)(2,1)S(1)}, bf16[384,1536]{1,0:T(8,128)(2,1)}, u32[]{:S(2)}) %copy-start.1) | copy-done | bytes 1179672
  7.0 0.0 copy-start.2
  7.0 1.0 %copy-done.2 = bf16[1,128,1536]{2,1,0:T(8,128)(2,1)S(1)} copy-done((bf16[1,128,1536]{2,1,0:T(8,128)(2,1)S(1)}, bf16[1,128,1536]{2,1,0:T(8,128)(2,1)}, u32[]{:S(2)}) %copy-start.2) | copy-done | bytes 393240
  8.0 0.0 copy-start.3
  8.0 0.9 copy-done.3
  8.9 0.0 copy-start.4
  8.9 0.9 copy-done.4
  9.8 0.0 copy-start.5
  9.8 0.9 copy-done.5
  10.7 0.0 copy-start.6
  10.7 0.8 copy-done.6
  11.5 0.0 copy-start.7
  11.5 0.7 copy-done.7
  12.1 82.4 %shard_map.131 = (bf16[128,128]{1,0:T(8,128)(2,1)S(1)}, f32[128,1]{1,0:T(8,128)S(1)}) custom-call(s32[1]{0:T(128)S(6)} %copy.16.visible, s32[128,1]{1,0:T(8,128)S(1)} %copy.15.keep_col, s32[1,128]{1,0:T(1,128)S(1)} %copy-done.7, bf16[128,1536]{1,0:T(8,128)(2,1)S(1)} %bitcast.4, bf16[128,128]{1,0:T(8,128)(2,1)S(1)} %pad.8.targets, ...), custom_call_target="tpu_custom_call" | custom-call | tf_op jit(solution)/shard_map/pallas_call | solution.py:358
  94.5 0.6 reduce.1
  95.2 0.7 reshape.26
  (1 shorter events, 0.0 us)
Async XLA Ops:
  4.5 1.3 %copy-start = (bf16[1536,384]{1,0:T(8,128)(2,1)S(1)}, bf16[1536,384]{1,0:T(8,128)(2,1)}, u32[]{:S(2)}) copy-start(bf16[1536,384]{1,0:T(8,128)(2,1)} %w_up.1) | copy-start | bytes 3538948
  5.7 1.3 %copy-start.1 = (bf16[384,1536]{1,0:T(8,128)(2,1)S(1)}, bf16[384,1536]{1,0:T(8,128)(2,1)}, u32[]{:S(2)}) copy-start(bf16[384,1536]{1,0:T(8,128)(2,1)} %w_down.1) | copy-start | bytes 3538948
  7.0 1.0 %copy-start.2 = (bf16[1,128,1536]{2,1,0:T(8,128)(2,1)S(1)}, bf16[1,128,1536]{2,1,0:T(8,128)(2,1)}, u32[]{:S(2)}) copy-start(bf16[1,128,1536]{2,1,0:T(8,128)(2,1)} %param.12) | copy-start | bytes 1179652
  8.0 0.9 copy-start.3
  8.9 0.9 copy-start.4
  9.8 0.9 copy-start.5
  10.7 0.8 copy-start.6
  11.5 0.7 copy-start.7

commit v2 on v1

--- a/solution.py
+++ b/solution.py
@@ -29,7 +29,6 @@
 PACKED = 1024
 
 UP_PIECE = 48
-DOWN_PIECE = 144
 CHUNKS = ((0, 48), (48, 32))
 
 
@@ -52,9 +51,10 @@
 
 
 def kernel(
-    visible, keep_col, keep_row, patches, targets, mask_token, position,
+    visible_hbm, keep_hbm, patches_hbm, targets_hbm, mask_hbm, position_hbm,
     w_up, w_down, d_embed, d_qkv, d_out, d_pred,
     recon, loss,
+    visible, keep, patches, targets, mask_token, position, pred,
     up, down, packed, up2, down2, dec, raw, slots, hidden, w2e, part, own, ret_out, ret_in, proj, mixed,
     load_sem, w_send, w_recv, d_send, d_recv, r_send, r_recv, b_send, b_recv,
 ):
@@ -79,39 +79,48 @@
     ahead, behind = at_z(sign), at_z(-sign)
 
     barrier = pltpu.get_barrier_semaphore()
-    greeted = [at_z(s) for s in (1, 2, 3, 4, 8, 12, 15)]
-    greeted += [at_x(s) for s in (1, 2, 3)] + [at_y(s) for s in (1, 2, 3)] + [other_core]
-    greeted_back = [at_z(s) for s in (13, 14)]
-    for device in greeted + greeted_back:
+    greeted = [at_z(s) for s in (8, 4, 12, 3, 13, 2, 14, 1, 15)]
+    greeted += [at_x(s) for s in (2, 1, 3)] + [at_y(s) for s in (2, 1, 3)] + [other_core]
+    for device in greeted:
         pl.semaphore_signal(barrier, inc=1, device_id=device, device_id_type=MESH)
 
-    loads = []
+    n_loads = [0]
 
     def load(src, dst):
-        copy = pltpu.make_async_copy(src, dst, load_sem.at[len(loads)])
+        copy = pltpu.make_async_copy(src, dst, load_sem.at[n_loads[0]])
+        n_loads[0] += 1
         copy.start()
-        loads.append(copy)
-
-    for j in range(4):
-        load(d_embed.at[:, pl.ds(j * LANES, LANES)], packed.at[pl.ds(EMBED_AT + j * 96, 96)])
-    for j in range(12):
-        load(d_qkv.at[:, pl.ds(j * LANES, LANES)], packed.at[pl.ds(QKV_AT + j * 32, 32)])
-    for j in range(4):
-        load(d_out.at[:, pl.ds(j * LANES, LANES)], packed.at[pl.ds(OUT_AT + j * 32, 32)])
-    load(d_pred, packed.at[pl.ds(PRED_AT, 32)])
-    load(w_up, up)
-    for j in range(12):
-        load(w_down.at[:, pl.ds(j * LANES, LANES)], down.at[pl.ds(j * SHARD, SHARD)])
-    packed[pl.ds(PRED_AT + 32, PACKED - PRED_AT - 32), :] = jnp.zeros((PACKED - PRED_AT - 32, LANES), BF16)
-
-    chosen = keep_col[0:VMAX, :] == lax.broadcasted_iota(jnp.int32, (VMAX, N_PATCH), 1)
-    picked = dot(chosen.astype(F32).astype(BF16), patches[...])
+        return copy
+
+    first_loads = [load(keep_hbm, keep), load(patches_hbm.at[0], patches)]
+    pack_loads = [
+        load(d_embed.at[:, pl.ds(j * LANES, LANES)], packed.at[pl.ds(EMBED_AT + j * 96, 96)]) for j in range(4)
+    ]
+    pack_loads += [
+        load(d_qkv.at[:, pl.ds(j * LANES, LANES)], packed.at[pl.ds(QKV_AT + j * 32, 32)]) for j in range(12)
+    ]
+    pack_loads += [
+        load(d_out.at[:, pl.ds(j * LANES, LANES)], packed.at[pl.ds(OUT_AT + j * 32, 32)]) for j in range(4)
+    ]
+    pack_loads += [load(d_pred, pred)]
+    up_load, down_load = load(w_up, up), load(w_down, down)
+    late_loads = [
+        load(visible_hbm, visible), load(targets_hbm, targets), load(mask_hbm, mask_token), load(position_hbm, position)
+    ]
+
+    for copy in first_loads:
+        copy.wait()
+    patch_of = lax.broadcasted_iota(jnp.int32, (N_PATCH, N_PATCH), 0)
+    chosen = jnp.where(keep[...] == patch_of, 1.0, 0.0)
+    picked = dot(jnp.transpose(chosen)[0:VMAX, :].astype(BF16), patches[...])
     raw[...] = picked.astype(BF16)
     slots[0] = layer_norm(picked).astype(BF16)
 
-    for copy in loads:
+    for copy in pack_loads:
         copy.wait()
-    pl.semaphore_wait(barrier, len(greeted) + len(greeted_back))
+    packed[pl.ds(PRED_AT, 32), :] = jnp.concatenate([pred[...], jnp.zeros((32, LANES - PIX), BF16)], axis=1)
+    packed[pl.ds(PRED_AT + 32, PACKED - PRED_AT - 32), :] = jnp.zeros((PACKED - PRED_AT - 32, LANES), BF16)
+    pl.semaphore_wait(barrier, len(greeted))
 
     def send(src, dst, sems, index, device):
         copy = pltpu.make_async_remote_copy(
@@ -137,14 +146,12 @@
     def up_at(piece, count):
         return pl.ds(pl.multiple_of(piece * UP_PIECE, 16), count * UP_PIECE)
 
-    def down_at(piece, count):
-        return pl.ds(pl.multiple_of(piece * DOWN_PIECE, 16), count * DOWN_PIECE)
-
+    def group(i, count):
+        return pl.ds(pl.multiple_of(i * 48, 16), count * 48)
+
+    cell = (group(c * 4 + x, 1), pl.ds(pl.multiple_of(y * SHARD, LANES), SHARD))
     w0 = send_all(
-        [
-            (up.at[up_at(q_x, 1)], up2.at[up_at(q_x, 1)], at_z(8)),
-            (down.at[down_at(q_y, 1)], down2.at[down_at(q_y, 1)], at_z(8)),
-        ],
+        [(w_up.at[up_at(q_x, 1)], up2.at[up_at(q_x, 1)], at_z(8)), (w_down.at[cell], down2.at[cell], at_z(8))],
         wsem, 0,
     )
 
@@ -157,17 +164,18 @@
         [(packed.at[rows_at(q_z, 1)], dec.at[mine, rows_at(q_z, 1)], at_z(s)) for s in (4, 8, 12)], dsem, 0
     )
 
+    def slot_of(k, side):
+        return 0 if k == 0 else (7 if k == 4 else 2 * k - 1 + side)
+
     def send_rows(k, side):
-        first = 0 if side == 0 else 3
-        src = 0 if k == 1 else first + k - 1
-        dst = first + k
+        src, dst = slot_of(k - 1, side), slot_of(k, side)
         return [
             (slots.at[src, pl.ds(at, n)], slots.at[dst, pl.ds(at, n)], ahead if side == 0 else behind)
             for at, n in CHUNKS
         ]
 
     def row_sem(k, side):
-        return 2 * ((0 if side == 0 else 3) + k - 1)
+        return 2 * (slot_of(k, side) - 1)
 
     rows = {}
 
@@ -187,9 +195,12 @@
 
     start_rows(1, 0)
     start_rows(1, 1)
-
-    def hide(slot):
-        hidden[slot, :, 0:SHARD] = gelu(dot(slots[slot], up[...])).astype(BF16)
+    up_load.wait()
+
+    def hide(slot, count=1):
+        block = slots[slot : slot + count].reshape(count * VMAX, D)
+        part = gelu(dot(block, up[...])).astype(BF16)
+        hidden[slot : slot + count, :, 0:SHARD] = part.reshape(count, VMAX, SHARD)
 
     hide(0)
 
@@ -203,11 +214,10 @@
     arrive(w0)
     w1 = send_all(
         [(up2.at[up_at(q_x, 1)], up2.at[up_at(q_x, 1)], at_x(s)) for s in (1, 2, 3)]
-        + [(down2.at[down_at(q_y, 1)], down2.at[down_at(q_y, 1)], at_y(s)) for s in (1, 2, 3)],
+        + [(down2.at[cell], down2.at[cell], at_y(s)) for s in (1, 2, 3)],
         wsem, 2,
     )
-    hide(1)
-    hide(4)
+    hide(1, 2)
 
     arrive(d1)
     low, high = pl.ds(0, 8), pl.ds(8, 8)
@@ -221,13 +231,12 @@
     q_xs, q_ys = c * 16 + y * 4, c * 16 + x * 4
     w2 = send_all(
         [(up2.at[up_at(q_xs, 4)], up2.at[up_at(q_xs, 4)], at_y(s)) for s in (1, 2, 3)]
-        + [(down2.at[down_at(q_ys, 4)], down2.at[down_at(q_ys, 4)], at_x(s)) for s in (1, 2, 3)],
+        + [(down2.at[group(c * 4 + x, 1)], down2.at[group(c * 4 + x, 1)], at_x(s)) for s in (1, 2, 3)],
         wsem, 8,
     )
 
     pass_rows(2)
-    hide(2)
-    hide(5)
+    hide(3, 2)
 
     arrive(d2)
     d3 = send_all(
@@ -240,14 +249,13 @@
     w3 = send_all(
         [
             (up2.at[up_at(c * 16, 16)], up2.at[up_at(c * 16, 16)], other_core),
-            (down2.at[down_at(c * 16, 16)], down2.at[down_at(c * 16, 16)], other_core),
+            (down2.at[group(c * 4, 4)], down2.at[group(c * 4, 4)], other_core),
         ],
         wsem, 14,
     )
 
     pass_rows(3)
-    hide(3)
-    hide(6)
+    hide(5, 2)
 
     arrive(d3)
     d4 = send_all([(dec.at[:, rows_at(c * 16, 16)], dec.at[:, rows_at(c * 16, 16)], other_core)], dsem, 18)
@@ -263,33 +271,35 @@
             axis=1,
         )
 
+    down_load.wait()
+    for copy in late_loads:
+        copy.wait()
     pass_rows(4)
     hide(7)
     arrive(w3)
 
-    def hide_far(slot, carry):
-        hidden[slot, :, SHARD : 2 * SHARD] = gelu(dot(slots[slot], up2[...])).astype(BF16)
+    def hide_far(i, carry):
+        block = slots[pl.ds(2 * i, 2)].reshape(2 * VMAX, D)
+        part = gelu(dot(block, up2[...])).astype(BF16)
+        hidden[pl.ds(2 * i, 2), :, SHARD : 2 * SHARD] = part.reshape(2, VMAX, SHARD)
         return carry
 
-    lax.fori_loop(0, 8, hide_far, 0)
+    lax.fori_loop(0, 4, hide_far, 0)
 
     arrive(d4)
-    downs = [
-        jnp.concatenate([ref[j * SHARD : (j + 1) * SHARD, :] for j in range(12)], axis=1) for ref in (down, down2)
-    ]
     for half in (0, 1):
         embed = weight(EMBED_AT, 96, (2 * half, 2 * half + 1))
         cols = slice(256 * half, 256 * half + 256)
-        for s in (0, 1):
-            w2e[s * SHARD : (s + 1) * SHARD, cols] = dot(downs[s], embed).astype(BF16)
+        for s, shard in enumerate((down, down2)):
+            w2e[s * SHARD : (s + 1) * SHARD, cols] = dot(shard[...], embed).astype(BF16)
         own[:, cols] = dot(raw[...], embed)
 
     def partial(slot):
         return dot(hidden[slot], w2e[...])
 
-    ret_out[3] = partial(7).astype(BF16)
+    ret_out[3] = partial(slot_of(4, 1)).astype(BF16)
     back = {(1, 0): send_all([(ret_out.at[3], ret_in.at[3], ahead)], bsem, 3)}
-    ret_out[0] = partial(3).astype(BF16)
+    ret_out[0] = partial(slot_of(3, 0)).astype(BF16)
     back[0, 0] = send_all([(ret_out.at[0], ret_in.at[0], behind)], bsem, 0)
     own[...] += partial(0)
 
@@ -300,30 +310,34 @@
     lax.fori_loop(1, 7, add_part, 0)
     for step in (0, 1, 2):
         arrive(back[1, step])
-        ret_out[4 + step] = (ret_in[3 + step].astype(F32) + part[6 - step]).astype(BF16)
+        ret_out[4 + step] = (ret_in[3 + step].astype(F32) + part[slot_of(3 - step, 1)]).astype(BF16)
         back[1, step + 1] = send_all([(ret_out.at[4 + step], ret_in.at[4 + step], ahead)], bsem, 4 + step)
         if step < 2:
             arrive(back[0, step])
-            ret_out[1 + step] = (ret_in[step].astype(F32) + part[2 - step]).astype(BF16)
+            ret_out[1 + step] = (ret_in[step].astype(F32) + part[slot_of(2 - step, 0)]).astype(BF16)
             back[0, step + 1] = send_all([(ret_out.at[1 + step], ret_in.at[1 + step], behind)], bsem, 1 + step)
+
+    count = visible[0]
+    row = lax.broadcasted_iota(jnp.int32, (N_PATCH, N_PATCH), 0)
+    lane = lax.broadcasted_iota(jnp.int32, (N_PATCH, N_PATCH), 1)
+    patch = 4 * (row % 32) + row // 32
+    spread = jnp.where((keep[...] == patch) & (lane < count), 1.0, 0.0)
+    seen = jnp.sum(spread, axis=1, keepdims=True) > 0.5
+    spread = spread[:, 0:VMAX].astype(BF16)
+    order = jnp.where(lane == patch, 1.0, 0.0)
+    places = dot(order.astype(BF16), position[...])
+    masked = mask_token[...].astype(F32).reshape(1, DD)
+
     arrive(back[0, 2])
     arrive(back[1, 3])
     embedded = (own[...] + ret_in[2].astype(F32) + ret_in[6].astype(F32)).astype(BF16)
-
-    count = visible[0]
-    spread = (keep_row[...] == lax.broadcasted_iota(jnp.int32, (N_PATCH, N_PATCH), 0)) & (
-        lax.broadcasted_iota(jnp.int32, (N_PATCH, N_PATCH), 1) < count
-    )
-    spread = jnp.where(spread, 1.0, 0.0)
-    seen = jnp.sum(spread, axis=1, keepdims=True) > 0.5
-    placed = dot(spread[:, 0:VMAX].astype(BF16), embedded)
-    start = jnp.where(seen, placed, mask_token[...].astype(F32)) + position[...].astype(F32)
+    start = jnp.where(seen, dot(spread, embedded), masked) + places
     normed = layer_norm(start).astype(BF16)
     for b in range(6):
         both = dot(normed, weight(QKV_AT, 32, (2 * b, 2 * b + 1))).astype(BF16)
         proj[2 * b] = both[:, 0:LANES]
         proj[2 * b + 1] = both[:, LANES : 2 * LANES]
-    left = lax.broadcasted_iota(jnp.int32, (N_PATCH, LANES), 1) < HSIZE
+    left = lane < HSIZE
     for b in range(4):
         query, keys, values = proj[b], proj[4 + b], proj[8 + b]
         outs = []
@@ -340,10 +354,25 @@
     )
     final = layer_norm(after).astype(BF16)
     prediction = dot(final, weight(PRED_AT, 32, (0,)))
-    recon[...] = prediction.astype(BF16)
-    error = prediction - targets[...].astype(F32)
-    error = jnp.sum(error * error, axis=-1, keepdims=True) * (1.0 / PIX)
-    loss[...] = jnp.where(seen, 0.0, error)
+
+    turned = [pltpu.roll(prediction[32 * r : 32 * r + 32, :], (PIX * r) % LANES, 1) if r else prediction[0:32, :] for r in range(4)]
+    lane = lane[0:32, :]
+    edges = (96, 64, 32)
+    pixels = [jnp.where(lane < edges[b], turned[b], turned[b + 1]) for b in range(3)]
+    sums = [0.0] * 4
+    for b in range(3):
+        wide = pixels[b].astype(BF16)
+        wanted = []
+        for g in range(32):
+            at = slice(384 * g + LANES * b, 384 * g + LANES * b + LANES)
+            recon[:, at] = wide[g : g + 1, :]
+            wanted.append(targets[:, at])
+        error = pixels[b] - jnp.concatenate(wanted, axis=0).astype(F32)
+        error = error * error
+        sums[b] += jnp.sum(jnp.where(lane < edges[b], error, 0.0), axis=-1, keepdims=True)
+        sums[b + 1] += jnp.sum(jnp.where(lane < edges[b], 0.0, error), axis=-1, keepdims=True)
+    per_row = jnp.where(seen, 0.0, jnp.concatenate(sums, axis=0) * (1.0 / PIX))
+    loss[...] = jnp.sum(order * per_row, axis=0, keepdims=True)
 
     for copy in sent:
         copy.wait_send()
@@ -352,23 +381,30 @@
 def body(
     patches, keep_index, visible, targets, w_up, w_down, dec_embed, dec_qkv, dec_out, dec_pred, mask_token, position
 ):
-    any_spec = pl.BlockSpec(memory_space=pl.ANY)
+    hbm = pl.BlockSpec(memory_space=pltpu.HBM)
     vmem = pl.BlockSpec(memory_space=pltpu.VMEM)
     dma = pltpu.SemaphoreType.DMA
-    recon, loss = pl.pallas_call(
+    return pl.pallas_call(
         kernel,
         out_shape=(
-            jax.ShapeDtypeStruct((N_PATCH, LANES), BF16),
-            jax.ShapeDtypeStruct((N_PATCH, 1), F32),
+            jax.ShapeDtypeStruct((1, N_PATCH * PIX), BF16),
+            jax.ShapeDtypeStruct((1, N_PATCH), F32),
         ),
-        in_specs=[pl.BlockSpec(memory_space=pltpu.SMEM)] + [vmem] * 6 + [any_spec] * 6,
+        in_specs=[hbm] * 12,
         out_specs=(vmem, vmem),
         scratch_shapes=[
+            pltpu.SMEM((1,), jnp.int32),
+            pltpu.VMEM((1, N_PATCH), jnp.int32),
+            pltpu.VMEM((N_PATCH, D), BF16),
+            pltpu.VMEM((1, N_PATCH * PIX), BF16),
+            pltpu.VMEM((DD,), BF16),
+            pltpu.VMEM((N_PATCH, DD), BF16),
+            pltpu.VMEM((32, PIX), BF16),
             pltpu.VMEM((D, SHARD), BF16),
-            pltpu.VMEM((12 * SHARD, LANES), BF16),
+            pltpu.VMEM((SHARD, D), BF16),
             pltpu.VMEM((PACKED, LANES), BF16),
             pltpu.VMEM((D, SHARD), BF16),
-            pltpu.VMEM((12 * SHARD, LANES), BF16),
+            pltpu.VMEM((SHARD, D), BF16),
             pltpu.VMEM((NZ, PACKED, LANES), BF16),
             pltpu.VMEM((VMAX, D), BF16),
             pltpu.VMEM((8, VMAX, D), BF16),
@@ -380,7 +416,7 @@
             pltpu.VMEM((7, VMAX, DD), BF16),
             pltpu.VMEM((12, N_PATCH, LANES), BF16),
             pltpu.VMEM((N_PATCH, DD), BF16),
-            dma((34,)),
+            dma((29,)),
             dma((16,)),
             dma((16,)),
             dma((19,)),
@@ -391,24 +427,12 @@
             dma((7,)),
         ],
         compiler_params=pltpu.CompilerParams(
-            collective_id=0, has_side_effects=True, vmem_limit_bytes=48 * 1024 * 1024
+            collective_id=0, has_side_effects=True, vmem_limit_bytes=56 * 1024 * 1024
         ),
     )(
-        visible,
-        keep_index.reshape(N_PATCH, 1),
-        keep_index,
-        patches.reshape(N_PATCH, D),
-        jnp.pad(targets.reshape(N_PATCH, PIX), ((0, 0), (0, LANES - PIX))),
-        mask_token.reshape(1, DD),
-        position,
-        w_up,
-        w_down,
-        dec_embed,
-        dec_qkv,
-        dec_out,
-        jnp.pad(dec_pred, ((0, 0), (0, LANES - PIX))),
-    )
-    return (recon[:, :PIX].reshape(1, N_PATCH * PIX), loss.reshape(1, N_PATCH))
+        visible, keep_index, patches, targets, mask_token, position,
+        w_up, w_down, dec_embed, dec_qkv, dec_out, dec_pred,
+    )
 
 
 def solution(mesh):

time: 96.4 us -> 87.3 us (0.906)
  local copies, waits for them, and re-layouts: 10.6 us -> 2.61 us
  other arithmetic: 1.56 us -> 0 us
    unnamed x16 -> x2, local copies, waits for them, and re-layouts: 7.63 us -> 2.61 us
    reshape x4 -> x0, local copies, waits for them, and re-layouts: 2.27 us -> none  [the longest x1 0.76 us: body(): keep_index.reshape(N_PATCH, 1)]
where the time goes in v2:
time: 87.3 us; the launch traced here: 87.1 us
  Pallas kernels  83.2 us (95%)
  local copies, waits for them, and re-layouts  2.61 us (3%)
  between operations  1.29 us (1%)
    pallas_call x1, Pallas kernels, body(): pl.pallas_call(kernel, out_shape=(jax.ShapeDtypeStruct((1, N_PATCH * PIX)...  83.2 us
    unnamed x2, local copies, waits for them, and re-layouts  2.61 us

profile of v2, /device:TPU:1, one launch (start us, length us, event | category | flops | bytes accessed | tf_op | source)
XLA Modules:
  0.0 87.1 jit_solution(135436398427588227)
XLA Ops:
  1.3 83.2 %shard_map.131 = (bf16[1,12288]{1,0:T(2,128)(2,1)}, f32[1,128]{1,0:T(1,128)}) custom-call(s32[1]{0:T(128)S(6)} %copy.16.visible_hbm, s32[1,128]{1,0:T(1,128)} %keep_hbm.1, bf16[1,128,1536]{2,1,0:T(8,128)(2,1)} %patches_hbm.1, bf16[1,12288]{1,0:T(2,128)(2,1)} %targets_hbm.1, bf16[512]{0:T(512)(128)(2,1)} %mask_hbm.1, bf16[128,512]{1,0:T(8,128)(2,1)} %position_hbm.1, ...), custom_call_target="tpu_custom_call" | custom-call | tf_op jit(solution)/shard_map/pallas_call | solution.py:387
  84.5 1.5 %copy.17 = bf16[1,12288]{1,0:T(2,128)(2,1)} copy(bf16[1,12288]{1,0:T(2,128)(2,1)} %get-tuple-element.4) | data formatting | bytes 49152
  86.0 1.1 %copy.18 = f32[1,128]{1,0:T(1,128)} copy(f32[1,128]{1,0:T(1,128)} %get-tuple-element.5) | data formatting | bytes 1024

commit v3 on v2

--- a/solution.py
+++ b/solution.py
@@ -23,10 +23,11 @@
 BF16 = jnp.bfloat16
 
 EMBED_AT = 0
-QKV_AT = 384
-OUT_AT = 768
-PRED_AT = 896
+PRED_AT = 384
+QKV_AT = 512
+OUT_AT = 896
 PACKED = 1024
+HALF = 512
 
 UP_PIECE = 48
 CHUNKS = ((0, 48), (48, 32))
@@ -65,6 +66,7 @@
     q_y = c * 16 + x * 4 + y
     cls = z % 4
     q_z = jnp.where(cls < 2, q_x, q_y)
+    q_xs, q_ys = c * 16 + y * 4, c * 16 + x * 4
 
     def at_z(step):
         return (dp, (z + step + 2 * NZ) % NZ)
@@ -119,7 +121,7 @@
     for copy in pack_loads:
         copy.wait()
     packed[pl.ds(PRED_AT, 32), :] = jnp.concatenate([pred[...], jnp.zeros((32, LANES - PIX), BF16)], axis=1)
-    packed[pl.ds(PRED_AT + 32, PACKED - PRED_AT - 32), :] = jnp.zeros((PACKED - PRED_AT - 32, LANES), BF16)
+    packed[pl.ds(PRED_AT + 32, HALF - PRED_AT - 32), :] = jnp.zeros((HALF - PRED_AT - 32, LANES), BF16)
     pl.semaphore_wait(barrier, len(greeted))
 
     def send(src, dst, sems, index, device):
@@ -155,14 +157,38 @@
         wsem, 0,
     )
 
-    def rows_at(piece, count):
-        return pl.ds(pl.multiple_of(piece * 32, 32), count * 32)
-
     mine = z_slot(z)
-    dec[mine, rows_at(q_z, 1), :] = packed[rows_at(q_z, 1), :]
-    d0 = send_all(
-        [(packed.at[rows_at(q_z, 1)], dec.at[mine, rows_at(q_z, 1)], at_z(s)) for s in (4, 8, 12)], dsem, 0
-    )
+    same_class = pl.ds(pl.multiple_of(cls * 4, 4), 4)
+    low, high = pl.ds(0, 8), pl.ds(8, 8)
+    gathers = {}
+
+    def gather(half, step):
+        def at(piece, count):
+            return pl.ds(pl.multiple_of(half * HALF + piece * 16, 16), count * 16)
+
+        def same(slots_z, rows_p, device):
+            return (dec.at[slots_z, rows_p], dec.at[slots_z, rows_p], device)
+
+        if step:
+            arrive(gathers[half, step - 1])
+        if step == 0:
+            dec[mine, at(q_z, 1), :] = packed[at(q_z, 1), :]
+            items = [(packed.at[at(q_z, 1)], dec.at[mine, at(q_z, 1)], at_z(s)) for s in (4, 8, 12)]
+        elif step == 1:
+            items = [same(same_class, at(q_z, 1), at_z(s)) for s in (1, 2, 3)]
+        elif step == 2:
+            items = [same(low, at(q_x, 1), at_x(s)) for s in (1, 2, 3)]
+            items += [same(high, at(q_y, 1), at_y(s)) for s in (1, 2, 3)]
+        elif step == 3:
+            items = [same(low, at(q_xs, 4), at_y(s)) for s in (1, 2, 3)]
+            items += [same(high, at(q_ys, 4), at_x(s)) for s in (1, 2, 3)]
+        elif step == 4:
+            items = [(dec.at[:, at(c * 16, 16)], dec.at[:, at(c * 16, 16)], other_core)]
+        else:
+            return
+        gathers[half, step] = send_all(items, dsem, half * 19 + (0, 3, 6, 12, 18)[step])
+
+    gather(0, 0)
 
     def slot_of(k, side):
         return 0 if k == 0 else (7 if k == 4 else 2 * k - 1 + side)
@@ -193,73 +219,6 @@
                 if side in items:
                     rows[k + 1, side] += send_all([items[side][i]], rsem, row_sem(k + 1, side) + i)
 
-    start_rows(1, 0)
-    start_rows(1, 1)
-    up_load.wait()
-
-    def hide(slot, count=1):
-        block = slots[slot : slot + count].reshape(count * VMAX, D)
-        part = gelu(dot(block, up[...])).astype(BF16)
-        hidden[slot : slot + count, :, 0:SHARD] = part.reshape(count, VMAX, SHARD)
-
-    hide(0)
-
-    arrive(d0)
-    block = pl.ds(pl.multiple_of(cls * 4, 4), 4)
-    d1 = send_all(
-        [(dec.at[block, rows_at(q_z, 1)], dec.at[block, rows_at(q_z, 1)], at_z(s)) for s in (1, 2, 3)], dsem, 3
-    )
-
-    pass_rows(1)
-    arrive(w0)
-    w1 = send_all(
-        [(up2.at[up_at(q_x, 1)], up2.at[up_at(q_x, 1)], at_x(s)) for s in (1, 2, 3)]
-        + [(down2.at[cell], down2.at[cell], at_y(s)) for s in (1, 2, 3)],
-        wsem, 2,
-    )
-    hide(1, 2)
-
-    arrive(d1)
-    low, high = pl.ds(0, 8), pl.ds(8, 8)
-    d2 = send_all(
-        [(dec.at[low, rows_at(q_x, 1)], dec.at[low, rows_at(q_x, 1)], at_x(s)) for s in (1, 2, 3)]
-        + [(dec.at[high, rows_at(q_y, 1)], dec.at[high, rows_at(q_y, 1)], at_y(s)) for s in (1, 2, 3)],
-        dsem, 6,
-    )
-
-    arrive(w1)
-    q_xs, q_ys = c * 16 + y * 4, c * 16 + x * 4
-    w2 = send_all(
-        [(up2.at[up_at(q_xs, 4)], up2.at[up_at(q_xs, 4)], at_y(s)) for s in (1, 2, 3)]
-        + [(down2.at[group(c * 4 + x, 1)], down2.at[group(c * 4 + x, 1)], at_x(s)) for s in (1, 2, 3)],
-        wsem, 8,
-    )
-
-    pass_rows(2)
-    hide(3, 2)
-
-    arrive(d2)
-    d3 = send_all(
-        [(dec.at[low, rows_at(q_xs, 4)], dec.at[low, rows_at(q_xs, 4)], at_y(s)) for s in (1, 2, 3)]
-        + [(dec.at[high, rows_at(q_ys, 4)], dec.at[high, rows_at(q_ys, 4)], at_x(s)) for s in (1, 2, 3)],
-        dsem, 12,
-    )
-
-    arrive(w2)
-    w3 = send_all(
-        [
-            (up2.at[up_at(c * 16, 16)], up2.at[up_at(c * 16, 16)], other_core),
-            (down2.at[group(c * 4, 4)], down2.at[group(c * 4, 4)], other_core),
-        ],
-        wsem, 14,
-    )
-
-    pass_rows(3)
-    hide(5, 2)
-
-    arrive(d3)
-    d4 = send_all([(dec.at[:, rows_at(c * 16, 16)], dec.at[:, rows_at(c * 16, 16)], other_core)], dsem, 18)
-
     def weight(at, rows_per, blocks):
         return jnp.concatenate(
             [
@@ -271,12 +230,10 @@
             axis=1,
         )
 
-    down_load.wait()
-    for copy in late_loads:
-        copy.wait()
-    pass_rows(4)
-    hide(7)
-    arrive(w3)
+    def hide(slot, count=1):
+        block = slots[slot : slot + count].reshape(count * VMAX, D)
+        part = gelu(dot(block, up[...])).astype(BF16)
+        hidden[slot : slot + count, :, 0:SHARD] = part.reshape(count, VMAX, SHARD)
 
     def hide_far(i, carry):
         block = slots[pl.ds(2 * i, 2)].reshape(2 * VMAX, D)
@@ -284,23 +241,80 @@
         hidden[pl.ds(2 * i, 2), :, SHARD : 2 * SHARD] = part.reshape(2, VMAX, SHARD)
         return carry
 
-    lax.fori_loop(0, 4, hide_far, 0)
-
-    arrive(d4)
+    start_rows(1, 0)
+    start_rows(1, 1)
+    up_load.wait()
+    hide(0)
+    gather(0, 1)
+    pass_rows(1)
+    arrive(w0)
+    w1 = send_all(
+        [(up2.at[up_at(q_x, 1)], up2.at[up_at(q_x, 1)], at_x(s)) for s in (1, 2, 3)]
+        + [(down2.at[cell], down2.at[cell], at_y(s)) for s in (1, 2, 3)],
+        wsem, 2,
+    )
+    gather(0, 2)
+    pass_rows(2)
+    arrive(w1)
+    w2 = send_all(
+        [(up2.at[up_at(q_xs, 4)], up2.at[up_at(q_xs, 4)], at_y(s)) for s in (1, 2, 3)]
+        + [(down2.at[group(c * 4 + x, 1)], down2.at[group(c * 4 + x, 1)], at_x(s)) for s in (1, 2, 3)],
+        wsem, 8,
+    )
+    gather(0, 3)
+    hide(1, 2)
+    pass_rows(3)
+    hide(3, 2)
+    gather(1, 0)
+    hide(5, 2)
+    gather(1, 1)
+    down_load.wait()
+    for copy in late_loads:
+        copy.wait()
+    arrive(w2)
+    w3 = send_all(
+        [
+            (up2.at[up_at(c * 16, 16)], up2.at[up_at(c * 16, 16)], other_core),
+            (down2.at[group(c * 4, 4)], down2.at[group(c * 4, 4)], other_core),
+        ],
+        wsem, 14,
+    )
+    gather(0, 4)
+    gather(1, 2)
+    arrive(w3)
+    lax.fori_loop(0, 3, hide_far, 0)
+    gather(0, 5)
     for half in (0, 1):
         embed = weight(EMBED_AT, 96, (2 * half, 2 * half + 1))
         cols = slice(256 * half, 256 * half + 256)
         for s, shard in enumerate((down, down2)):
             w2e[s * SHARD : (s + 1) * SHARD, cols] = dot(shard[...], embed).astype(BF16)
         own[:, cols] = dot(raw[...], embed)
+    pass_rows(4)
+    hide(7)
+    hide_far(3, 0)
+    gather(1, 3)
 
     def partial(slot):
         return dot(hidden[slot], w2e[...])
 
-    ret_out[3] = partial(slot_of(4, 1)).astype(BF16)
-    back = {(1, 0): send_all([(ret_out.at[3], ret_in.at[3], ahead)], bsem, 3)}
-    ret_out[0] = partial(slot_of(3, 0)).astype(BF16)
-    back[0, 0] = send_all([(ret_out.at[0], ret_in.at[0], behind)], bsem, 0)
+    back = {}
+    wide = DD // 2
+
+    def hand_back(side, step, value):
+        i = side * 3 + step
+        to = behind if side == 0 else ahead
+        back[side, step] = []
+        for h in (0, 1):
+            if step:
+                arrive([back[side, step - 1][h]])
+                ret_out[i, h] = (ret_in[i - 1, h].astype(F32) + part[value, :, h * wide : (h + 1) * wide]).astype(BF16)
+            else:
+                ret_out[i, h] = value[:, h * wide : (h + 1) * wide].astype(BF16)
+            back[side, step] += send_all([(ret_out.at[i, h], ret_in.at[i, h], to)], bsem, 2 * i + h)
+
+    hand_back(1, 0, partial(slot_of(4, 1)))
+    hand_back(0, 0, partial(slot_of(3, 0)))
     own[...] += partial(0)
 
     def add_part(slot, carry):
@@ -308,14 +322,11 @@
         return carry
 
     lax.fori_loop(1, 7, add_part, 0)
-    for step in (0, 1, 2):
-        arrive(back[1, step])
-        ret_out[4 + step] = (ret_in[3 + step].astype(F32) + part[slot_of(3 - step, 1)]).astype(BF16)
-        back[1, step + 1] = send_all([(ret_out.at[4 + step], ret_in.at[4 + step], ahead)], bsem, 4 + step)
-        if step < 2:
-            arrive(back[0, step])
-            ret_out[1 + step] = (ret_in[step].astype(F32) + part[slot_of(2 - step, 0)]).astype(BF16)
-            back[0, step + 1] = send_all([(ret_out.at[1 + step], ret_in.at[1 + step], behind)], bsem, 1 + step)
+    for step in (1, 2, 3):
+        hand_back(1, step, slot_of(4 - step, 1))
+        if step < 3:
+            hand_back(0, step, slot_of(3 - step, 0))
+    gather(1, 4)
 
     count = visible[0]
     row = lax.broadcasted_iota(jnp.int32, (N_PATCH, N_PATCH), 0)
@@ -330,7 +341,9 @@
 
     arrive(back[0, 2])
     arrive(back[1, 3])
-    embedded = (own[...] + ret_in[2].astype(F32) + ret_in[6].astype(F32)).astype(BF16)
+    returned = [ret_in[2, h].astype(F32) + ret_in[6, h].astype(F32) for h in (0, 1)]
+    embedded = (own[...] + jnp.concatenate(returned, axis=1)).astype(BF16)
+    gather(1, 5)
     start = jnp.where(seen, dot(spread, embedded), masked) + places
     normed = layer_norm(start).astype(BF16)
     for b in range(6):
@@ -412,19 +425,19 @@
             pltpu.VMEM((2 * SHARD, DD), BF16),
             pltpu.VMEM((8, VMAX, DD), F32),
             pltpu.VMEM((VMAX, DD), F32),
-            pltpu.VMEM((7, VMAX, DD), BF16),
-            pltpu.VMEM((7, VMAX, DD), BF16),
+            pltpu.VMEM((7, 2, VMAX, DD // 2), BF16),
+            pltpu.VMEM((7, 2, VMAX, DD // 2), BF16),
             pltpu.VMEM((12, N_PATCH, LANES), BF16),
             pltpu.VMEM((N_PATCH, DD), BF16),
             dma((29,)),
             dma((16,)),
             dma((16,)),
-            dma((19,)),
-            dma((19,)),
+            dma((38,)),
+            dma((38,)),
             dma((14,)),
             dma((14,)),
-            dma((7,)),
-            dma((7,)),
+            dma((14,)),
+            dma((14,)),
         ],
         compiler_params=pltpu.CompilerParams(
             collective_id=0, has_side_effects=True, vmem_limit_bytes=56 * 1024 * 1024

time: 87.3 us -> 83.6 us (0.958)
  Pallas kernels: 83.2 us -> 79.5 us
    pallas_call x1, Pallas kernels: 83.2 us -> 79.5 us  [body(): pl.pallas_call(kernel, out_shape=(jax.ShapeDtypeStruct((1, N_PATCH * PIX)...]
where the time goes in v3:
time: 83.6 us; the launch traced here: 83.4 us
  Pallas kernels  79.5 us (95%)
  local copies, waits for them, and re-layouts  2.61 us (3%)
  between operations  1.29 us (2%)
    pallas_call x1, Pallas kernels, body(): pl.pallas_call(kernel, out_shape=(jax.ShapeDtypeStruct((1, N_PATCH * PIX)...  79.5 us
    unnamed x2, local copies, waits for them, and re-layouts  2.61 us

profile of v3, /device:TPU:1, one launch (start us, length us, event | category | flops | bytes accessed | tf_op | source)
XLA Modules:
  0.0 83.4 jit_solution(8912774255211409203)
XLA Ops:
  1.3 79.5 %shard_map.131 = (bf16[1,12288]{1,0:T(2,128)(2,1)}, f32[1,128]{1,0:T(1,128)}) custom-call(s32[1]{0:T(128)S(6)} %copy.16.visible_hbm, s32[1,128]{1,0:T(1,128)} %keep_hbm.1, bf16[1,128,1536]{2,1,0:T(8,128)(2,1)} %patches_hbm.1, bf16[1,12288]{1,0:T(2,128)(2,1)} %targets_hbm.1, bf16[512]{0:T(512)(128)(2,1)} %mask_hbm.1, bf16[128,512]{1,0:T(8,128)(2,1)} %position_hbm.1, ...), custom_call_target="tpu_custom_call" | custom-call | tf_op jit(solution)/shard_map/pallas_call | solution.py:400
  80.8 1.5 %copy.17 = bf16[1,12288]{1,0:T(2,128)(2,1)} copy(bf16[1,12288]{1,0:T(2,128)(2,1)} %get-tuple-element.4) | data formatting | bytes 49152
  82.2 1.1 %copy.18 = f32[1,128]{1,0:T(1,128)} copy(f32[1,128]{1,0:T(1,128)} %get-tuple-element.5) | data formatting | bytes 1024

commit v4 on v3

--- a/solution.py
+++ b/solution.py
@@ -262,12 +262,12 @@
         wsem, 8,
     )
     gather(0, 3)
+    gather(1, 0)
     hide(1, 2)
     pass_rows(3)
+    gather(1, 1)
     hide(3, 2)
-    gather(1, 0)
     hide(5, 2)
-    gather(1, 1)
     down_load.wait()
     for copy in late_loads:
         copy.wait()
@@ -374,11 +374,10 @@
     pixels = [jnp.where(lane < edges[b], turned[b], turned[b + 1]) for b in range(3)]
     sums = [0.0] * 4
     for b in range(3):
-        wide = pixels[b].astype(BF16)
+        recon[:, LANES * b : LANES * b + LANES] = pixels[b].astype(BF16)
         wanted = []
         for g in range(32):
             at = slice(384 * g + LANES * b, 384 * g + LANES * b + LANES)
-            recon[:, at] = wide[g : g + 1, :]
             wanted.append(targets[:, at])
         error = pixels[b] - jnp.concatenate(wanted, axis=0).astype(F32)
         error = error * error
@@ -397,10 +396,10 @@
     hbm = pl.BlockSpec(memory_space=pltpu.HBM)
     vmem = pl.BlockSpec(memory_space=pltpu.VMEM)
     dma = pltpu.SemaphoreType.DMA
-    return pl.pallas_call(
+    recon, loss = pl.pallas_call(
         kernel,
         out_shape=(
-            jax.ShapeDtypeStruct((1, N_PATCH * PIX), BF16),
+            jax.ShapeDtypeStruct((32, 4 * PIX), BF16),
             jax.ShapeDtypeStruct((1, N_PATCH), F32),
         ),
         in_specs=[hbm] * 12,
@@ -446,6 +445,7 @@
         visible, keep_index, patches, targets, mask_token, position,
         w_up, w_down, dec_embed, dec_qkv, dec_out, dec_pred,
     )
+    return (recon.reshape(1, N_PATCH * PIX), loss)
 
 
 def solution(mesh):

time: 83.6 us -> 81.8 us (0.978)
  Pallas kernels: 79.5 us -> 77.7 us
    pallas_call x1, Pallas kernels: 79.5 us -> 77.7 us  [body(): pl.pallas_call(kernel, out_shape=(jax.ShapeDtypeStruct((32, 4 * PIX), BF1...]
where the time goes in v4:
time: 81.8 us; the launch traced here: 81.6 us
  Pallas kernels  77.7 us (95%)
  local copies, waits for them, and re-layouts  2.57 us (3%)
  between operations  1.29 us (2%)
    pallas_call x1, Pallas kernels, body(): pl.pallas_call(kernel, out_shape=(jax.ShapeDtypeStruct((32, 4 * PIX), BF1...  77.7 us
    unnamed x2, local copies, waits for them, and re-layouts  2.57 us

profile of v4, /device:TPU:1, one launch (start us, length us, event | category | flops | bytes accessed | tf_op | source)
XLA Modules:
  0.0 81.6 jit_solution(3292367381025824236)
XLA Ops:
  1.3 77.7 %shard_map.131 = (bf16[32,384]{1,0:T(8,128)(2,1)}, f32[1,128]{1,0:T(1,128)}) custom-call(s32[1]{0:T(128)S(6)} %copy.16.visible_hbm, s32[1,128]{1,0:T(1,128)} %keep_hbm.1, bf16[1,128,1536]{2,1,0:T(8,128)(2,1)} %patches_hbm.1, bf16[1,12288]{1,0:T(2,128)(2,1)} %targets_hbm.1, bf16[512]{0:T(512)(128)(2,1)} %mask_hbm.1, bf16[128,512]{1,0:T(8,128)(2,1)} %position_hbm.1, ...), custom_call_target="tpu_custom_call" | custom-call | tf_op jit(solution)/shard_map/pallas_call | solution.py:399
  79.0 1.4 %copy.14 = bf16[1,1,32,384]{3,1,2,0:T(2,128)(2,1)} copy(bf16[1,1,32,384]{3,2,1,0:T(8,128)(2,1)} %bitcast.4) | data formatting | bytes 49152
  80.4 1.2 %copy.17 = f32[1,128]{1,0:T(1,128)} copy(f32[1,128]{1,0:T(1,128)} %get-tuple-element.9) | data formatting | bytes 1024
